TPU v7x, 256 devices: a whole 4x4x8 slice. The times are simulated.
256 devices in a mesh: dp: 16 (over z, core), ctx: 4 (over x), head: 4 (over y).
Axes of the slice: x: 4, y: 4, z: 8, core: 2. Of those that a mesh axis runs over, the one named last changes fastest.
Arguments:
- hidden_in: bfloat16 [16, 2048, 8192], P('dp', 'ctx', 'head'), may hold values from -40 to 40
- w_query: bfloat16 [8192, 4096], P('dp', 'head'), may hold values from -0.0625 to 0.0625
- w_key: bfloat16 [8192, 512], P('dp', 'head'), may hold values from -0.0625 to 0.0625
- w_value: bfloat16 [8192, 512], P('dp', 'head'), may hold values from -0.0625 to 0.0625
- mem_gate: float32 [32], P('head'), may hold values from -3 to 3
Outputs:
- attended: bfloat16 [16, 2048, 4096], P('dp', 'ctx', 'head')
All inputs are finite; a program needn't handle non-finite values.
Results may differ from a plain program's by a relative error of at most 0.011.
Values may be sent and summed in bfloat16 or wider, within the bound.
A program may use at most 128 MiB of HBM per device.

v0:
```python
import math

import jax
import jax.numpy as jnp
from jax import lax
from jax.experimental import pallas as pl
from jax.experimental.pallas import tpu as pltpu
from jax.sharding import PartitionSpec as P

HD = 128
SEG = 128
GROUP = 8
RINGZ = 8
RING = 4
ROWS = 512
COMMON = 192
QUARTER = 80
COLS = 1280
TOK = 512
FEAT = 2048
MESH = pl.DeviceIdType.MESH
LIMIT = 52 << 20
F32 = jnp.float32
BF16 = jnp.bfloat16


def kernel(
    hidden, w_query, w_key, w_value, sq, base, memory,
    w_all, h_all, acc, memaug, state, prior, before,
    load_sem, zq_s, zq_r, za_s, za_r, xq_s, xq_r, xf_s, xf_r,
    c_s, c_r, y_s, y_r, yf_s, yf_r, st_s, st_r,
):
    dp = lax.axis_index("dp")
    x = lax.axis_index("ctx")
    y = lax.axis_index("head")
    z, core = dp // 2, dp % 2

    def zdev(step):
        return {"dp": (z + RINGZ + step) % RINGZ * 2 + core}

    def xdev(step):
        return {"ctx": (x + RING + step) % RING}

    def ydev(step):
        return {"head": (y + RING + step) % RING}

    other = {"dp": z * 2 + 1 - core}
    SIGN = (1, -1)

    started = []

    def send(src, dst, ssem, rsem, dev):
        copy = pltpu.make_async_remote_copy(
            src_ref=src, dst_ref=dst, send_sem=ssem, recv_sem=rsem,
            device_id=dev, device_id_type=MESH,
        )
        copy.start()
        started.append(copy)

    def arrived(dst, ssem, rsem):
        pltpu.make_async_remote_copy(
            src_ref=dst, dst_ref=dst, send_sem=ssem, recv_sem=rsem,
            device_id=other, device_id_type=MESH,
        ).wait_recv()

    def block_of(step):
        return (z + RINGZ + step) % RINGZ * 2 + core

    def wrows(block, start, size):
        return w_all.at[pl.ds(pl.multiple_of(block * ROWS + start, 16), size), :]

    own = pl.multiple_of(dp * ROWS, ROWS)
    loads = [
        pltpu.make_async_copy(w_query, w_all.at[pl.ds(own, ROWS), 0:1024], load_sem.at[0]),
        pltpu.make_async_copy(w_key, w_all.at[pl.ds(own, ROWS), 1024:1152], load_sem.at[1]),
        pltpu.make_async_copy(w_value, w_all.at[pl.ds(own, ROWS), 1152:1280], load_sem.at[2]),
    ]
    loads.append(pltpu.make_async_copy(hidden.at[0], h_all.at[y], load_sem.at[3]))
    for load in loads:
        load.start()

    barrier = pltpu.get_barrier_semaphore()
    for peer in (zdev(1), zdev(-1), xdev(1), xdev(-1), xdev(2), ydev(1), ydev(-1), other):
        pl.semaphore_signal(barrier, inc=1, device_id=peer, device_id_type=MESH)
    pl.semaphore_wait(barrier, 8)

    def hrows(shard, start, size):
        return h_all.at[shard, pl.ds(start, size), :]

    def y_own(direction, segment):
        rows = segment * SEG, SEG
        send(
            hidden.at[0, pl.ds(*rows), :], hrows(y, *rows),
            y_s.at[direction, segment], y_r.at[direction, segment], ydev(SIGN[direction]),
        )

    def y_half(shard, direction, segment):
        return hrows(shard, segment * SEG + direction * SEG // 2, SEG // 2)

    def y_arrived(direction, segment):
        shard = (y + RING - SIGN[direction]) % RING
        arrived(
            hrows(shard, segment * SEG, SEG),
            y_s.at[direction, segment], y_r.at[direction, segment],
        )
        half = y_half(shard, direction, segment)
        send(
            half, half, yf_s.at[direction, segment], yf_r.at[direction, segment],
            ydev(SIGN[direction]),
        )

    def y_far(direction, segment):
        half = y_half((y + 2) % RING, direction, segment)
        arrived(half, yf_s.at[direction, segment], yf_r.at[direction, segment])

    for segment in range(4):
        y_own(0, segment), y_own(1, segment)

    def q_part(block, part, half):
        start, size = ((0, QUARTER), (0, 48), (48, 32))[half]
        return wrows(block, COMMON + part * QUARTER + start, size)

    def a_part(block, direction, step, piece):
        if step == 4:
            return wrows(block, direction * COMMON // 2, COMMON // 2)
        return wrows(block, (piece, 2 - piece)[direction] * COMMON // 3, COMMON // 3)

    def z_half(direction, step):
        return 0 if step < 4 else 1 + direction

    def zq_send(direction, step):
        block = block_of(-SIGN[direction] * (step - 1))
        part = q_part(block, x, z_half(direction, step))
        send(part, part, zq_s.at[direction, step - 1], zq_r.at[direction, step - 1], zdev(SIGN[direction]))

    def za_send(direction, step, piece):
        part = a_part(block_of(-SIGN[direction] * (step - 1)), direction, step, piece)
        sems = za_s.at[direction, step - 1, piece], za_r.at[direction, step - 1, piece]
        send(part, part, *sems, zdev(SIGN[direction]))

    def zq_arrived(direction, step):
        part = q_part(block_of(-SIGN[direction] * step), x, z_half(direction, step))
        arrived(part, zq_s.at[direction, step - 1], zq_r.at[direction, step - 1])
        if step < 4:
            zq_send(direction, step + 1)
        if step < 3:
            za_send(direction, 1, step)

    def za_arrived(direction, step, piece):
        part = a_part(block_of(-SIGN[direction] * step), direction, step, piece)
        sems = za_s.at[direction, step - 1, piece], za_r.at[direction, step - 1, piece]
        arrived(part, *sems)
        if step < 3:
            za_send(direction, step + 1, piece)
        elif step == 3 and piece == 1:
            za_send(direction, 4, 0)

    def x_block(i):
        return block_of((-1, 1, -2, 2, -3, 3, 4)[i])

    def xq_send(i):
        part = q_part(x_block(i), x, 0)
        for direction in (0, 1):
            send(part, part, xq_s.at[i, direction], xq_r.at[i, direction], xdev(SIGN[direction]))

    def xq_arrived(i):
        for direction in (0, 1):
            source = (x + RING - SIGN[direction]) % RING
            whole = q_part(x_block(i), source, 0)
            arrived(whole, xq_s.at[i, direction], xq_r.at[i, direction])
            part = q_part(x_block(i), source, 1 + direction)
            send(part, part, xf_s.at[i, direction], xf_r.at[i, direction], xdev(SIGN[direction]))

    def c_send(i):
        block = dp if i == 7 else x_block(i)
        part = wrows(block, 0, ROWS)
        send(part, part, c_s.at[i], c_r.at[i], other)

    def xf_arrived(i):
        for direction in (0, 1):
            part = q_part(x_block(i), (x + 2) % RING, 1 + direction)
            arrived(part, xf_s.at[i, direction], xf_r.at[i, direction])

    def c_arrived(i):
        block = dp if i == 7 else x_block(i)
        part = wrows(block + 1 - 2 * core, 0, ROWS)
        arrived(part, c_s.at[i], c_r.at[i])

    far = (y + 2) % RING

    def multiply(row, rows, block, start=0, size=COLS):
        column = pl.multiple_of(block % 4 * ROWS, ROWS)
        acc[row:row + rows, start:start + size] += jnp.dot(
            h_all[block // 4, row:row + rows, pl.ds(column, ROWS)],
            w_all[pl.ds(pl.multiple_of(block * ROWS, ROWS), ROWS), start:start + size],
            preferred_element_type=F32,
        )

    def multiply_near(step, first, last):
        def one(i, carry):
            block = (z + RINGZ + (1 - i // 2 * 2) * step) % RINGZ * 2 + i % 2

            @pl.when(block // 4 != far)
            def _():
                multiply(0, TOK, block)

            return carry

        lax.fori_loop(first, last, one, 0)

    def multiply_far(row, rows, first=0, last=4, start=0, size=COLS):
        def one(i, carry):
            multiply(row, rows, far * 4 + i, start, size)
            return carry

        lax.fori_loop(first, last, one, 0)

    def feature(v):
        return jnp.where(v > 0, v + 1.0, jnp.exp(jnp.minimum(v, 0.0)))

    iota_q = lax.broadcasted_iota(jnp.int32, (SEG, SEG), 0)
    iota_k = lax.broadcasted_iota(jnp.int32, (SEG, SEG), 1)
    scale = 1.0 / math.sqrt(HD)

    def keys_of(segment):
        rows = slice(segment * SEG, (segment + 1) * SEG)
        return acc[rows, 1024:1152].astype(BF16), acc[rows, 1152:1280].astype(BF16)

    def increment(segment):
        keys, values = keys_of(segment)
        wide = feature(keys.astype(F32))
        high = wide.astype(BF16)
        low = (wide - high.astype(F32)).astype(BF16)
        left = jnp.concatenate([values.astype(F32).T.astype(BF16), jnp.ones((HD, SEG), BF16)], axis=0)
        added = jnp.dot(left, high, preferred_element_type=F32) + jnp.dot(
            left, low, preferred_element_type=F32
        )
        memaug[segment + 1] = memaug[segment] + added

    def local(segment):
        rows = slice(segment * SEG, (segment + 1) * SEG)
        keys, values = keys_of(segment)
        values = jnp.concatenate([values, jnp.ones((SEG, HD), BF16)], axis=1)
        for h in range(GROUP):
            cols = slice(h * HD, (h + 1) * HD)
            query = acc[rows, cols].astype(BF16)
            scores = lax.dot_general(
                query, keys, (((1,), (1,)), ((), ())), preferred_element_type=F32
            ) * scale
            scores = jnp.where(iota_q >= iota_k, scores, -jnp.inf)
            top = jnp.max(scores, axis=1, keepdims=True)
            probs = jnp.exp(scores - top).astype(BF16)
            both = jnp.dot(probs, values, preferred_element_type=F32)
            base[rows, cols] = both[:, :HD] / both[:, HD:]
            sq[rows, cols] = feature(query.astype(F32)).astype(BF16)

    def state_copy(j):
        return pltpu.make_async_remote_copy(
            src_ref=state, dst_ref=prior.at[j - 1], send_sem=st_s.at[j - 1], recv_sem=st_r.at[j - 1],
            device_id=xdev(j), device_id_type=MESH,
        )

    def both_ways(f, *n):
        f(0, *n), f(1, *n)

    for load in loads:
        load.wait()
    both_ways(zq_send, 1)
    both_ways(za_send, 1, 0)
    c_send(7)
    acc[...] = jnp.zeros_like(acc)
    memaug[0] = jnp.zeros((2 * HD, HD), F32)
    before[...] = jnp.zeros_like(before)

    both_ways(zq_arrived, 1)
    xq_send(0), xq_send(1)
    xq_arrived(0)
    both_ways(zq_arrived, 2)
    xq_send(2), xq_send(3)
    xq_arrived(1)
    both_ways(zq_arrived, 3)
    both_ways(za_arrived, 1, 0)
    both_ways(za_arrived, 1, 1)
    xq_send(4), xq_send(5)
    xq_arrived(2)
    both_ways(y_arrived, 0)
    xf_arrived(0)
    both_ways(za_arrived, 1, 2)
    c_send(0)
    both_ways(y_arrived, 1)
    both_ways(zq_arrived, 4)
    xq_send(6)
    xq_arrived(3)
    xf_arrived(1)
    c_send(1)
    both_ways(za_arrived, 2, 0)
    both_ways(za_arrived, 2, 1)
    xq_arrived(4)
    both_ways(y_arrived, 2)
    both_ways(za_arrived, 2, 2)
    xq_arrived(5)
    xf_arrived(2), xf_arrived(3)
    c_send(2), c_send(3)
    both_ways(za_arrived, 3, 0)
    both_ways(za_arrived, 3, 1)
    xq_arrived(6)
    both_ways(y_arrived, 3)
    for i in (7, 0, 1):
        c_arrived(i)
    multiply_near(0, 0, 2)
    multiply_near(1, 0, 2)
    both_ways(za_arrived, 3, 2)
    xf_arrived(4), xf_arrived(5)
    c_send(4), c_send(5)
    multiply_near(1, 2, 4)
    c_arrived(2), c_arrived(3)
    multiply_near(2, 0, 2)
    both_ways(za_arrived, 4, 0)
    xf_arrived(6)
    c_send(6)
    multiply_near(2, 2, 4)
    c_arrived(4), c_arrived(5)
    multiply_near(3, 0, 4)
    c_arrived(6)
    multiply_near(4, 0, 2)
    both_ways(y_far, 0), both_ways(y_far, 1)
    multiply_far(0, 256)
    for segment in (0, 1):
        increment(segment)
        local(segment)
    both_ways(y_far, 2)
    multiply_far(256, 128)
    increment(2)
    local(2)
    both_ways(y_far, 3)
    multiply_far(384, 128, 0, 4, 1024, 256)
    increment(3)
    state[...] = memaug[4, :HD + 16].astype(BF16)
    multiply_far(384, 128, 0, 1, 0, 1024)
    for j in (1, 2, 3):
        @pl.when(x + j < RING)
        def _():
            state_copy(j).start()
    multiply_far(384, 128, 1, 4, 0, 1024)
    local(3)
    for j in (1, 2, 3):
        @pl.when(x >= j)
        def _():
            state_copy(j).wait_recv()
            before[:HD] += prior[j - 1, :HD].astype(F32)
            before[HD:] += prior[j - 1, HD:HD + 1].astype(F32)
    for segment in range(4):
        memory[segment] = (memaug[segment] + before[...]).astype(BF16)
    for copy in started:
        copy.wait_send()
    for j in (1, 2, 3):
        @pl.when(x + j < RING)
        def _():
            state_copy(j).wait_send()


def share(gate, h):
    return jax.nn.sigmoid(jnp.full((1, HD), gate[h], F32))


def finish(sq, base, memory, gate, out):
    for h in range(GROUP):
        cols = slice(h * HD, (h + 1) * HD)
        both = lax.dot_general(
            sq[:, cols], memory[0], (((1,), (1,)), ((), ())), preferred_element_type=F32
        )
        part = share(gate, h)
        retrieved = both[:, :HD] / (both[:, HD:] + 1.0)
        out[0, :, cols] = (part * retrieved + (1.0 - part) * base[:, cols]).astype(BF16)


def body(hidden_in, w_query, w_key, w_value, mem_gate):
    dma = pltpu.SemaphoreType.DMA
    anywhere = pl.BlockSpec(memory_space=pl.ANY)
    width = GROUP * HD
    results = pl.pallas_call(
        kernel,
        out_shape=(
            pltpu.VMEM((TOK, width), BF16),
            pltpu.VMEM((TOK, width), F32),
            pltpu.VMEM((4, 2 * HD, HD), BF16),
        ),
        in_specs=[anywhere] * 4,
        out_specs=[pl.BlockSpec(memory_space=pltpu.VMEM)] * 3,
        scratch_shapes=[
            pltpu.VMEM((16 * ROWS, COLS), BF16),
            pltpu.VMEM((RING, TOK, FEAT), BF16),
            pltpu.VMEM((TOK, COLS), F32),
            pltpu.VMEM((5, 2 * HD, HD), F32),
            pltpu.VMEM((HD + 16, HD), BF16),
            pltpu.VMEM((3, HD + 16, HD), BF16),
            pltpu.VMEM((2 * HD, HD), F32),
            dma((4,)), dma((2, 4)), dma((2, 4)), dma((2, 4, 3)), dma((2, 4, 3)),
            dma((7, 2)), dma((7, 2)), dma((7, 2)), dma((7, 2)),
            dma((8,)), dma((8,)), dma((2, 4)), dma((2, 4)), dma((2, 4)), dma((2, 4)),
            dma((3,)), dma((3,)),
        ],
        compiler_params=pltpu.CompilerParams(
            collective_id=0, has_side_effects=True, vmem_limit_bytes=LIMIT
        ),
    )(*[pltpu.with_memory_space_constraint(a, pltpu.HBM) for a in (hidden_in, w_query, w_key, w_value)])
    return pl.pallas_call(
        finish,
        grid=(4,),
        out_shape=jax.ShapeDtypeStruct((1, TOK, width), BF16),
        in_specs=[
            pl.BlockSpec((SEG, width), lambda i: (i, 0)),
            pl.BlockSpec((SEG, width), lambda i: (i, 0)),
            pl.BlockSpec((1, 2 * HD, HD), lambda i: (i, 0, 0)),
            pl.BlockSpec(memory_space=pltpu.SMEM),
        ],
        out_specs=pl.BlockSpec((1, SEG, width), lambda i: (0, i, 0)),
        compiler_params=pltpu.CompilerParams(vmem_limit_bytes=8 << 20),
    )(*results, mem_gate)


def solution(mesh):
    return jax.shard_map(
        body,
        mesh=mesh,
        in_specs=(
            P("dp", "ctx", "head"),
            P("dp", "head"),
            P("dp", "head"),
            P("dp", "head"),
            P("head"),
        ),
        out_specs=P("dp", "ctx", "head"),
        check_vma=False,
    )
```

profile of v0, /device:TPU:16, one launch (start us, length us, event | category | flops | bytes accessed | tf_op | source)
XLA Modules:
  0.0 88.5 jit_solution(9277050843305722544)
XLA Ops:
  0.0 0.0 copy-start
  0.0 85.6 %shard_map.55 = (bf16[512,1024]{1,0:T(8,128)(2,1)S(1)}, f32[512,1024]{1,0:T(8,128)S(1)}, bf16[4,256,128]{2,1,0:T(8,128)(2,1)S(1)}) custom-call(bf16[1,512,2048]{2,1,0:T(8,128)(2,1)} %hidden.1, bf16[512,1024]{1,0:T(8,128)(2,1)} %w_query.1, bf16[512,128]{1,0:T(8,128)(2,1)} %w_key.1, bf16[512,128]{1,0:T(8,128)(2,1)} %w_value.1), custom_call_target="tpu_custom_call" | custom-call | tf_op jit(solution)/shard_map/pallas_call | solution.py:381
  85.6 0.0 copy-done
  85.6 2.9 %shard_map.56 = bf16[1,512,1024]{2,1,0:T(8,128)(2,1)} custom-call(bf16[512,1024]{1,0:T(8,128)(2,1)S(1)} %get-tuple-element.8.sq, f32[512,1024]{1,0:T(8,128)S(1)} %get-tuple-element.9.base, bf16[4,256,128]{2,1,0:T(8,128)(2,1)S(1)} %get-tuple-element.10.memory, f32[8]{0:T(128)S(1)} %copy-done), custom_call_target="tpu_custom_call" | custom-call | tf_op jit(solution)/shard_map/pallas_call | solution.py:407
Async XLA Ops:
  0.0 85.6 %copy-start = (f32[8]{0:T(128)S(1)}, f32[8]{0:T(128)}, u32[]{:S(2)}) copy-start(f32[8]{0:T(128)} %gate.1) | copy-start | bytes 100
where the time goes:
time: 88.6 us; the launch traced here: 88.5 us
  Pallas kernels  88.5 us (100%)
    pallas_call x1, Pallas kernels, body(): pl.pallas_call(kernel, out_shape=(pltpu.VMEM((TOK, width), BF16), pltpu.V...  85.6 us
    pallas_call x1, Pallas kernels, body(): pl.pallas_call(finish, grid=(4,), out_shape=jax.ShapeDtypeStruct((1, TOK,...  2.94 us

commit v1 on v0

--- a/solution.py
+++ b/solution.py
@@ -117,7 +117,7 @@
         y_own(0, segment), y_own(1, segment)
 
     def q_part(block, part, half):
-        start, size = ((0, QUARTER), (0, 48), (48, 32))[half]
+        start, size = ((0, QUARTER), (0, 48), (48, 32), (0, 32), (32, 48))[half]
         return wrows(block, COMMON + part * QUARTER + start, size)
 
     def a_part(block, direction, step, piece):
@@ -143,8 +143,8 @@
         arrived(part, zq_s.at[direction, step - 1], zq_r.at[direction, step - 1])
         if step < 4:
             zq_send(direction, step + 1)
-        if step < 3:
-            za_send(direction, 1, step)
+        if step == 1:
+            za_send(direction, 1, 2)
 
     def za_arrived(direction, step, piece):
         part = a_part(block_of(-SIGN[direction] * step), direction, step, piece)
@@ -168,23 +168,26 @@
             source = (x + RING - SIGN[direction]) % RING
             whole = q_part(x_block(i), source, 0)
             arrived(whole, xq_s.at[i, direction], xq_r.at[i, direction])
-            part = q_part(x_block(i), source, 1 + direction)
+            part = q_part(x_block(i), source, 1 + direction + i % 2 * 2)
             send(part, part, xf_s.at[i, direction], xf_r.at[i, direction], xdev(SIGN[direction]))
 
-    def c_send(i):
-        block = dp if i == 7 else x_block(i)
-        part = wrows(block, 0, ROWS)
-        send(part, part, c_s.at[i], c_r.at[i], other)
+    def c_part(block, part):
+        start, size = ((0, COMMON), (COMMON, ROWS - COMMON))[part]
+        return wrows(block, start, size)
+
+    def c_send(i, part):
+        rows = c_part(dp if i == 7 else x_block(i), part)
+        send(rows, rows, c_s.at[i, part], c_r.at[i, part], other)
 
     def xf_arrived(i):
         for direction in (0, 1):
-            part = q_part(x_block(i), (x + 2) % RING, 1 + direction)
+            part = q_part(x_block(i), (x + 2) % RING, 1 + direction + i % 2 * 2)
             arrived(part, xf_s.at[i, direction], xf_r.at[i, direction])
 
     def c_arrived(i):
         block = dp if i == 7 else x_block(i)
-        part = wrows(block + 1 - 2 * core, 0, ROWS)
-        arrived(part, c_s.at[i], c_r.at[i])
+        for part in (0, 1):
+            arrived(c_part(block + 1 - 2 * core, part), c_s.at[i, part], c_r.at[i, part])
 
     far = (y + 2) % RING
 
@@ -208,9 +211,17 @@
 
         lax.fori_loop(first, last, one, 0)
 
-    def multiply_far(row, rows, first=0, last=4, start=0, size=COLS):
+    opposite = (z + 4) % RINGZ
+
+    def multiply_far(row, rows, first=0, last=4, start=0, size=COLS, late=None):
         def one(i, carry):
-            multiply(row, rows, far * 4 + i, start, size)
+            block = far * 4 + i
+            if late is None:
+                multiply(row, rows, block, start, size)
+            else:
+                @pl.when((block // 2 == opposite) == late)
+                def _():
+                    multiply(row, rows, block, start, size)
             return carry
 
         lax.fori_loop(first, last, one, 0)
@@ -267,64 +278,69 @@
         load.wait()
     both_ways(zq_send, 1)
     both_ways(za_send, 1, 0)
-    c_send(7)
+    both_ways(za_send, 1, 1)
+    c_send(7, 0), c_send(7, 1)
     acc[...] = jnp.zeros_like(acc)
     memaug[0] = jnp.zeros((2 * HD, HD), F32)
     before[...] = jnp.zeros_like(before)
 
     both_ways(zq_arrived, 1)
     xq_send(0), xq_send(1)
+    both_ways(za_arrived, 1, 0)
     xq_arrived(0)
+    both_ways(y_arrived, 0)
+    xq_arrived(1)
     both_ways(zq_arrived, 2)
     xq_send(2), xq_send(3)
-    xq_arrived(1)
+    both_ways(za_arrived, 1, 1)
+    xf_arrived(0)
+    c_send(0, 1)
+    both_ways(za_arrived, 1, 2)
+    c_send(0, 0), c_send(1, 0)
+    xf_arrived(1)
+    c_send(1, 1)
+    both_ways(y_arrived, 1)
+    xq_arrived(2)
     both_ways(zq_arrived, 3)
-    both_ways(za_arrived, 1, 0)
-    both_ways(za_arrived, 1, 1)
+    xq_arrived(3)
     xq_send(4), xq_send(5)
-    xq_arrived(2)
-    both_ways(y_arrived, 0)
-    xf_arrived(0)
-    both_ways(za_arrived, 1, 2)
-    c_send(0)
-    both_ways(y_arrived, 1)
+    both_ways(za_arrived, 2, 0)
+    both_ways(za_arrived, 2, 1)
+    xf_arrived(2), xf_arrived(3)
+    c_send(2, 1), c_send(3, 1)
+    both_ways(za_arrived, 2, 2)
+    c_send(2, 0), c_send(3, 0)
+    both_ways(y_arrived, 2)
+    xq_arrived(4)
     both_ways(zq_arrived, 4)
     xq_send(6)
-    xq_arrived(3)
-    xf_arrived(1)
-    c_send(1)
-    both_ways(za_arrived, 2, 0)
-    both_ways(za_arrived, 2, 1)
-    xq_arrived(4)
-    both_ways(y_arrived, 2)
-    both_ways(za_arrived, 2, 2)
     xq_arrived(5)
-    xf_arrived(2), xf_arrived(3)
-    c_send(2), c_send(3)
     both_ways(za_arrived, 3, 0)
     both_ways(za_arrived, 3, 1)
+    xf_arrived(4), xf_arrived(5)
+    c_send(4, 1), c_send(5, 1)
+    both_ways(y_arrived, 3)
     xq_arrived(6)
-    both_ways(y_arrived, 3)
     for i in (7, 0, 1):
         c_arrived(i)
     multiply_near(0, 0, 2)
-    multiply_near(1, 0, 2)
     both_ways(za_arrived, 3, 2)
-    xf_arrived(4), xf_arrived(5)
-    c_send(4), c_send(5)
-    multiply_near(1, 2, 4)
+    c_send(4, 0), c_send(5, 0)
+    multiply_near(1, 0, 4)
+    xf_arrived(6)
+    c_send(6, 1)
     c_arrived(2), c_arrived(3)
     multiply_near(2, 0, 2)
     both_ways(za_arrived, 4, 0)
-    xf_arrived(6)
-    c_send(6)
+    c_send(6, 0)
     multiply_near(2, 2, 4)
     c_arrived(4), c_arrived(5)
     multiply_near(3, 0, 4)
+    both_ways(y_far, 0), both_ways(y_far, 1)
+    multiply_far(0, 256, late=False)
     c_arrived(6)
+    multiply_far(0, 256, late=True)
     multiply_near(4, 0, 2)
-    both_ways(y_far, 0), both_ways(y_far, 1)
-    multiply_far(0, 256)
     for segment in (0, 1):
         increment(segment)
         local(segment)
@@ -363,15 +379,22 @@
     return jax.nn.sigmoid(jnp.full((1, HD), gate[h], F32))
 
 
-def finish(sq, base, memory, gate, out):
-    for h in range(GROUP):
-        cols = slice(h * HD, (h + 1) * HD)
-        both = lax.dot_general(
-            sq[:, cols], memory[0], (((1,), (1,)), ((), ())), preferred_element_type=F32
-        )
-        part = share(gate, h)
-        retrieved = both[:, :HD] / (both[:, HD:] + 1.0)
-        out[0, :, cols] = (part * retrieved + (1.0 - part) * base[:, cols]).astype(BF16)
+def finish(sq, base, memory, gate, out, mixed, sem):
+    copies = []
+    for segment in range(TOK // SEG):
+        rows = slice(segment * SEG, (segment + 1) * SEG)
+        for h in range(GROUP):
+            cols = slice(h * HD, (h + 1) * HD)
+            both = lax.dot_general(
+                sq[rows, cols], memory[segment], (((1,), (1,)), ((), ())), preferred_element_type=F32
+            )
+            part = share(gate, h)
+            retrieved = both[:, :HD] / (both[:, HD:] + 1.0)
+            mixed[rows, cols] = (part * retrieved + (1.0 - part) * base[rows, cols]).astype(BF16)
+        copies.append(pltpu.make_async_copy(mixed.at[rows, :], out.at[0, rows, :], sem.at[segment]))
+        copies[-1].start()
+    for copy in copies:
+        copy.wait()
 
 
 def body(hidden_in, w_query, w_key, w_value, mem_gate):
@@ -397,24 +420,20 @@
             pltpu.VMEM((2 * HD, HD), F32),
             dma((4,)), dma((2, 4)), dma((2, 4)), dma((2, 4, 3)), dma((2, 4, 3)),
             dma((7, 2)), dma((7, 2)), dma((7, 2)), dma((7, 2)),
-            dma((8,)), dma((8,)), dma((2, 4)), dma((2, 4)), dma((2, 4)), dma((2, 4)),
+            dma((8, 2)), dma((8, 2)), dma((2, 4)), dma((2, 4)), dma((2, 4)), dma((2, 4)),
             dma((3,)), dma((3,)),
         ],
         compiler_params=pltpu.CompilerParams(
             collective_id=0, has_side_effects=True, vmem_limit_bytes=LIMIT
         ),
     )(*[pltpu.with_memory_space_constraint(a, pltpu.HBM) for a in (hidden_in, w_query, w_key, w_value)])
+    vmem = pl.BlockSpec(memory_space=pltpu.VMEM)
     return pl.pallas_call(
         finish,
-        grid=(4,),
         out_shape=jax.ShapeDtypeStruct((1, TOK, width), BF16),
-        in_specs=[
-            pl.BlockSpec((SEG, width), lambda i: (i, 0)),
-            pl.BlockSpec((SEG, width), lambda i: (i, 0)),
-            pl.BlockSpec((1, 2 * HD, HD), lambda i: (i, 0, 0)),
-            pl.BlockSpec(memory_space=pltpu.SMEM),
-        ],
-        out_specs=pl.BlockSpec((1, SEG, width), lambda i: (0, i, 0)),
+        in_specs=[vmem, vmem, vmem, pl.BlockSpec(memory_space=pltpu.SMEM)],
+        out_specs=anywhere,
+        scratch_shapes=[pltpu.VMEM((TOK, width), BF16), dma((4,))],
         compiler_params=pltpu.CompilerParams(vmem_limit_bytes=8 << 20),
     )(*results, mem_gate)
 

time: 88.6 us -> 86.5 us (0.976)
  Pallas kernels: 88.5 us -> 86.4 us
    pallas_call x1, Pallas kernels: 85.6 us -> 84.4 us  [body(): pl.pallas_call(kernel, out_shape=(pltpu.VMEM((TOK, width), BF16), pltpu.V...]
    pallas_call x1, Pallas kernels: 2.94 us -> 2 us  [body(): pl.pallas_call(finish, out_shape=jax.ShapeDtypeStruct((1, TOK, width), BF...]
where the time goes in v1:
time: 86.5 us; the launch traced here: 86.4 us
  Pallas kernels  86.4 us (100%)
    pallas_call x1, Pallas kernels, body(): pl.pallas_call(kernel, out_shape=(pltpu.VMEM((TOK, width), BF16), pltpu.V...  84.4 us
    pallas_call x1, Pallas kernels, body(): pl.pallas_call(finish, out_shape=jax.ShapeDtypeStruct((1, TOK, width), BF...  2 us

profile of v1, /device:TPU:16, one launch (start us, length us, event | category | flops | bytes accessed | tf_op | source)
XLA Modules:
  0.0 86.4 jit_solution(14373279151184497678)
XLA Ops:
  0.0 0.0 copy-start
  0.0 84.4 %shard_map.55 = (bf16[512,1024]{1,0:T(8,128)(2,1)S(1)}, f32[512,1024]{1,0:T(8,128)S(1)}, bf16[4,256,128]{2,1,0:T(8,128)(2,1)S(1)}) custom-call(bf16[1,512,2048]{2,1,0:T(8,128)(2,1)} %hidden.1, bf16[512,1024]{1,0:T(8,128)(2,1)} %w_query.1, bf16[512,128]{1,0:T(8,128)(2,1)} %w_key.1, bf16[512,128]{1,0:T(8,128)(2,1)} %w_value.1), custom_call_target="tpu_custom_call" | custom-call | tf_op jit(solution)/shard_map/pallas_call | solution.py:404
  84.4 0.0 copy-done
  84.4 2.0 %shard_map.56 = bf16[1,512,1024]{2,1,0:T(8,128)(2,1)} custom-call(bf16[512,1024]{1,0:T(8,128)(2,1)S(1)} %get-tuple-element.8.sq, f32[512,1024]{1,0:T(8,128)S(1)} %get-tuple-element.9.base, bf16[4,256,128]{2,1,0:T(8,128)(2,1)S(1)} %get-tuple-element.10.memory, f32[8]{0:T(128)S(1)} %copy-done), custom_call_target="tpu_custom_call" | custom-call | tf_op jit(solution)/shard_map/pallas_call | solution.py:431
Async XLA Ops:
  0.0 84.4 %copy-start = (f32[8]{0:T(128)S(1)}, f32[8]{0:T(128)}, u32[]{:S(2)}) copy-start(f32[8]{0:T(128)} %gate.1) | copy-start | bytes 100

commit v2 on v1

--- a/solution.py
+++ b/solution.py
@@ -47,15 +47,15 @@
     other = {"dp": z * 2 + 1 - core}
     SIGN = (1, -1)
 
-    started = []
-
-    def send(src, dst, ssem, rsem, dev):
+    started, forwarded = [], []
+
+    def send(src, dst, ssem, rsem, dev, held=None):
         copy = pltpu.make_async_remote_copy(
             src_ref=src, dst_ref=dst, send_sem=ssem, recv_sem=rsem,
             device_id=dev, device_id_type=MESH,
         )
         copy.start()
-        started.append(copy)
+        (started if held is None else held).append(copy)
 
     def arrived(dst, ssem, rsem):
         pltpu.make_async_remote_copy(
@@ -94,8 +94,11 @@
             y_s.at[direction, segment], y_r.at[direction, segment], ydev(SIGN[direction]),
         )
 
-    def y_half(shard, direction, segment):
-        return hrows(shard, segment * SEG + direction * SEG // 2, SEG // 2)
+    def y_half(shard, direction, piece):
+        if piece >= 3:
+            columns = pl.ds((2 * direction + piece - 3) * ROWS, ROWS)
+            return h_all.at[shard, pl.ds(3 * SEG, SEG), columns]
+        return hrows(shard, piece * SEG + direction * SEG // 2, SEG // 2)
 
     def y_arrived(direction, segment):
         shard = (y + RING - SIGN[direction]) % RING
@@ -103,15 +106,16 @@
             hrows(shard, segment * SEG, SEG),
             y_s.at[direction, segment], y_r.at[direction, segment],
         )
-        half = y_half(shard, direction, segment)
-        send(
-            half, half, yf_s.at[direction, segment], yf_r.at[direction, segment],
-            ydev(SIGN[direction]),
-        )
-
-    def y_far(direction, segment):
-        half = y_half((y + 2) % RING, direction, segment)
-        arrived(half, yf_s.at[direction, segment], yf_r.at[direction, segment])
+        for piece in (3, 4) if segment == 3 else (segment,):
+            half = y_half(shard, direction, piece)
+            send(
+                half, half, yf_s.at[direction, piece], yf_r.at[direction, piece],
+                ydev(SIGN[direction]), forwarded,
+            )
+
+    def y_far(direction, piece):
+        half = y_half((y + 2) % RING, direction, piece)
+        arrived(half, yf_s.at[direction, piece], yf_r.at[direction, piece])
 
     for segment in range(4):
         y_own(0, segment), y_own(1, segment)
@@ -232,6 +236,13 @@
     iota_q = lax.broadcasted_iota(jnp.int32, (SEG, SEG), 0)
     iota_k = lax.broadcasted_iota(jnp.int32, (SEG, SEG), 1)
     scale = 1.0 / math.sqrt(HD)
+
+    def multiply_last(first, last, odd, start, size):
+        def one(i, carry):
+            multiply(384, 128, far * 4 + 2 * i + odd, start, size)
+            return carry
+
+        lax.fori_loop(first, last, one, 0)
 
     def keys_of(segment):
         rows = slice(segment * SEG, (segment + 1) * SEG)
@@ -344,20 +355,24 @@
     for segment in (0, 1):
         increment(segment)
         local(segment)
+    for copy in started:
+        copy.wait_send()
     both_ways(y_far, 2)
     multiply_far(256, 128)
     increment(2)
-    local(2)
     both_ways(y_far, 3)
-    multiply_far(384, 128, 0, 4, 1024, 256)
+    multiply_last(0, 2, 0, 0, COLS)
+    both_ways(y_far, 4)
+    multiply_last(0, 2, 1, 1024, 256)
     increment(3)
     state[...] = memaug[4, :HD + 16].astype(BF16)
-    multiply_far(384, 128, 0, 1, 0, 1024)
+    multiply_last(0, 1, 1, 0, 1024)
     for j in (1, 2, 3):
         @pl.when(x + j < RING)
         def _():
             state_copy(j).start()
-    multiply_far(384, 128, 1, 4, 0, 1024)
+    multiply_last(1, 2, 1, 0, 1024)
+    local(2)
     local(3)
     for j in (1, 2, 3):
         @pl.when(x >= j)
@@ -367,7 +382,7 @@
             before[HD:] += prior[j - 1, HD:HD + 1].astype(F32)
     for segment in range(4):
         memory[segment] = (memaug[segment] + before[...]).astype(BF16)
-    for copy in started:
+    for copy in forwarded:
         copy.wait_send()
     for j in (1, 2, 3):
         @pl.when(x + j < RING)
@@ -420,7 +435,7 @@
             pltpu.VMEM((2 * HD, HD), F32),
             dma((4,)), dma((2, 4)), dma((2, 4)), dma((2, 4, 3)), dma((2, 4, 3)),
             dma((7, 2)), dma((7, 2)), dma((7, 2)), dma((7, 2)),
-            dma((8, 2)), dma((8, 2)), dma((2, 4)), dma((2, 4)), dma((2, 4)), dma((2, 4)),
+            dma((8, 2)), dma((8, 2)), dma((2, 4)), dma((2, 4)), dma((2, 5)), dma((2, 5)),
             dma((3,)), dma((3,)),
         ],
         compiler_params=pltpu.CompilerParams(

time: 86.5 us -> 86.1 us (level); the launches traced: 86.4 us -> 85.1 us
  Pallas kernels: 86.4 us -> 85.1 us
    pallas_call x1, Pallas kernels: 84.4 us -> 83.1 us  [body(): pl.pallas_call(kernel, out_shape=(pltpu.VMEM((TOK, width), BF16), pltpu.V...]
where the time goes in v2:
time: 86.1 us; the launch traced here: 85.1 us
  Pallas kernels  85.1 us (99%)
    pallas_call x1, Pallas kernels, body(): pl.pallas_call(kernel, out_shape=(pltpu.VMEM((TOK, width), BF16), pltpu.V...  83.1 us
    pallas_call x1, Pallas kernels, body(): pl.pallas_call(finish, out_shape=jax.ShapeDtypeStruct((1, TOK, width), BF...  2 us

profile of v2, /device:TPU:16, one launch (start us, length us, event | category | flops | bytes accessed | tf_op | source)
XLA Modules:
  0.0 85.1 jit_solution(13002062339940473092)
XLA Ops:
  0.0 0.0 copy-start
  0.0 83.1 %shard_map.55 = (bf16[512,1024]{1,0:T(8,128)(2,1)S(1)}, f32[512,1024]{1,0:T(8,128)S(1)}, bf16[4,256,128]{2,1,0:T(8,128)(2,1)S(1)}) custom-call(bf16[1,512,2048]{2,1,0:T(8,128)(2,1)} %hidden.1, bf16[512,1024]{1,0:T(8,128)(2,1)} %w_query.1, bf16[512,128]{1,0:T(8,128)(2,1)} %w_key.1, bf16[512,128]{1,0:T(8,128)(2,1)} %w_value.1), custom_call_target="tpu_custom_call" | custom-call | tf_op jit(solution)/shard_map/pallas_call | solution.py:419
  83.1 0.0 copy-done
  83.1 2.0 %shard_map.56 = bf16[1,512,1024]{2,1,0:T(8,128)(2,1)} custom-call(bf16[512,1024]{1,0:T(8,128)(2,1)S(1)} %get-tuple-element.8.sq, f32[512,1024]{1,0:T(8,128)S(1)} %get-tuple-element.9.base, bf16[4,256,128]{2,1,0:T(8,128)(2,1)S(1)} %get-tuple-element.10.memory, f32[8]{0:T(128)S(1)} %copy-done), custom_call_target="tpu_custom_call" | custom-call | tf_op jit(solution)/shard_map/pallas_call | solution.py:446
Async XLA Ops:
  0.0 83.1 %copy-start = (f32[8]{0:T(128)S(1)}, f32[8]{0:T(128)}, u32[]{:S(2)}) copy-start(f32[8]{0:T(128)} %gate.1) | copy-start | bytes 100

commit v3 on v2

--- a/solution.py
+++ b/solution.py
@@ -338,13 +338,13 @@
     both_ways(za_arrived, 3, 2)
     c_send(4, 0), c_send(5, 0)
     multiply_near(1, 0, 4)
+    c_arrived(2), c_arrived(3)
+    multiply_near(2, 0, 2)
     xf_arrived(6)
     c_send(6, 1)
-    c_arrived(2), c_arrived(3)
-    multiply_near(2, 0, 2)
+    multiply_near(2, 2, 4)
     both_ways(za_arrived, 4, 0)
     c_send(6, 0)
-    multiply_near(2, 2, 4)
     c_arrived(4), c_arrived(5)
     multiply_near(3, 0, 4)
     both_ways(y_far, 0), both_ways(y_far, 1)

time: 86.1 us -> 84.9 us (0.986)
  Pallas kernels: 85.1 us -> 83.3 us
    pallas_call x1, Pallas kernels: 83.1 us -> 81.3 us  [body(): pl.pallas_call(kernel, out_shape=(pltpu.VMEM((TOK, width), BF16), pltpu.V...]
where the time goes in v3:
time: 84.9 us; the launch traced here: 83.3 us
  Pallas kernels  83.3 us (98%)
    pallas_call x1, Pallas kernels, body(): pl.pallas_call(kernel, out_shape=(pltpu.VMEM((TOK, width), BF16), pltpu.V...  81.3 us
    pallas_call x1, Pallas kernels, body(): pl.pallas_call(finish, out_shape=jax.ShapeDtypeStruct((1, TOK, width), BF...  2 us

profile of v3, /device:TPU:16, one launch (start us, length us, event | category | flops | bytes accessed | tf_op | source)
XLA Modules:
  0.0 83.3 jit_solution(9211995145244494097)
XLA Ops:
  0.0 0.0 copy-start
  0.0 81.3 %shard_map.55 = (bf16[512,1024]{1,0:T(8,128)(2,1)S(1)}, f32[512,1024]{1,0:T(8,128)S(1)}, bf16[4,256,128]{2,1,0:T(8,128)(2,1)S(1)}) custom-call(bf16[1,512,2048]{2,1,0:T(8,128)(2,1)} %hidden.1, bf16[512,1024]{1,0:T(8,128)(2,1)} %w_query.1, bf16[512,128]{1,0:T(8,128)(2,1)} %w_key.1, bf16[512,128]{1,0:T(8,128)(2,1)} %w_value.1), custom_call_target="tpu_custom_call" | custom-call | tf_op jit(solution)/shard_map/pallas_call | solution.py:419
  81.3 0.0 copy-done
  81.3 2.0 %shard_map.56 = bf16[1,512,1024]{2,1,0:T(8,128)(2,1)} custom-call(bf16[512,1024]{1,0:T(8,128)(2,1)S(1)} %get-tuple-element.8.sq, f32[512,1024]{1,0:T(8,128)S(1)} %get-tuple-element.9.base, bf16[4,256,128]{2,1,0:T(8,128)(2,1)S(1)} %get-tuple-element.10.memory, f32[8]{0:T(128)S(1)} %copy-done), custom_call_target="tpu_custom_call" | custom-call | tf_op jit(solution)/shard_map/pallas_call | solution.py:446
Async XLA Ops:
  0.0 81.3 %copy-start = (f32[8]{0:T(128)S(1)}, f32[8]{0:T(128)}, u32[]{:S(2)}) copy-start(f32[8]{0:T(128)} %gate.1) | copy-start | bytes 100
